TPU v7x, 128 devices: a whole 4x4x4 slice. The times are simulated.
128 devices in a mesh: frame: 32 (over y, x, core), tile: 4 (over z).
Axes of the slice: x: 4, y: 4, z: 4, core: 2. Of those that a mesh axis runs over, the one named last changes fastest.
Arguments:
- counts: float32 [1024, 524288], P('frame', 'tile'), may hold values from -1 to 23
- dark_level: float32 [524288], P('tile'), may hold values from 0 to 2
- flat_field: float32 [524288], P('tile'), may hold values from 0.5 to 2
- valid_pixel: int32 [524288], P('tile'), may hold values 0 or 1
- cycle_label: int32 [524288], P('tile'), may hold values from 0 to 32, as said below
- cycle_order: int32 [4, 32, 32], P('tile'), may hold values from 0 to 1024, as said below
- age_bin: int32 [1024], replicated, may hold values from 0 to 15, never falling along the last dimension, each value on 1 to 128 neighbouring positions
Outputs:
- two_time: float32 [32, 1024, 1024], P('frame', 'tile')
- aged_correlation: float32 [32, 16, 1024], P('frame', None, 'tile')
- mean_image: float32 [4, 32, 4096], P('tile', 'frame')
Inputs may be any that keep to these rules, and one draw needn't show every extreme that they name: cycle_order[t, q, :] lists distinct pixel blocks of module t (indices within the module) whose nominal cycle is q, then 131072 // 128 in the unused entries; no block is listed twice in a module; some cycle fills all entries of each module. `cycle_label`: most pixels carry the nominal cycle of the block under which cycle_order lists them.
All inputs are finite; a program needn't handle non-finite values. No bound on the sum of `valid_pixel` on one device may be relied on, other than what follows from the above.
Results may differ from a plain program's by a relative error of at most 0.0003.
Values may be sent and summed in bfloat16 or wider, within the bound.
A program may use at most 128 MiB of HBM per device.

v0:
```python
import jax
import jax.numpy as jnp
from jax import lax
from jax.sharding import PartitionSpec as P

BLK = 128
NA = 16


def band_rows(cmap_rows, age_bin):
    cycle_count, row_count, col_width = cmap_rows.shape
    padded_map = jnp.concatenate([cmap_rows, jnp.zeros_like(cmap_rows)], axis=2)
    span = col_width + row_count
    flattened = jnp.concatenate(
        [
            padded_map.reshape(cycle_count, row_count * span),
            jnp.zeros((cycle_count, row_count), jnp.float32),
        ],
        axis=1,
    )
    skewed_map = flattened.reshape(cycle_count, row_count, span + 1)[:, :, :col_width]
    onehot = (age_bin[None, :] == jnp.arange(NA, dtype=jnp.int32)[:, None]).astype(jnp.float32)
    return jnp.einsum("bi,rid->rbd", onehot, skewed_map, precision=lax.Precision.HIGHEST)


def lag_counts(age_bin, lag_start, lag_count):
    frames = age_bin.shape[0]
    lag_values = lag_start + jnp.arange(lag_count, dtype=jnp.int32)
    inside = (jnp.arange(frames, dtype=jnp.int32)[:, None] + lag_values[None, :] < frames).astype(
        jnp.float32
    )
    onehot = (age_bin[None, :] == jnp.arange(NA, dtype=jnp.int32)[:, None]).astype(jnp.float32)
    return jnp.dot(onehot, inside, precision=lax.Precision.HIGHEST)


def gram_block(frame_block, exchanged):
    return jnp.einsum("irp,jrp->irj", frame_block, exchanged, preferred_element_type=jnp.float32)


def block_rows(values, block_ids, block_total):
    return jnp.take(values.reshape(block_total, BLK), block_ids, axis=0)


def local(counts, dark_level, flat_field, valid_pixel, cycle_label, cycle_order, age_bin):
    pix_module = dark_level.shape[0]
    block_total = pix_module // BLK
    block_order = cycle_order[0]
    cycle_total, block_count = block_order.shape
    slot = block_count * BLK
    frame_part = counts.shape[0]
    is_padding = (block_order >= block_total)[:, :, None]
    block_ids = jnp.where(block_order >= block_total, 0, block_order).reshape(-1)
    cycle_ids = jnp.arange(cycle_total, dtype=jnp.int32)[:, None, None]
    usable = (
        block_rows(valid_pixel, block_ids, block_total)
        .reshape(cycle_total, block_count, BLK)
        .astype(jnp.float32)
    )
    matching = (
        block_rows(cycle_label, block_ids, block_total).reshape(cycle_total, block_count, BLK)
        == cycle_ids
    ).astype(jnp.float32)
    member_blocks = jnp.where(is_padding, 0.0, usable * matching)
    member = member_blocks.reshape(cycle_total, slot)
    slot_gain = block_rows(flat_field, block_ids, block_total) * member_blocks.reshape(
        cycle_total * block_count, BLK
    )
    slot_dark = block_rows(dark_level, block_ids, block_total)
    columns = jnp.take(counts.reshape(frame_part, block_total, BLK), block_ids, axis=1)
    sorted_frames = (
        ((columns - slot_dark[None]) * slot_gain[None])
        .astype(jnp.bfloat16)
        .reshape(frame_part, cycle_total, slot)
    )
    exchanged = lax.all_to_all(sorted_frames, "frame", split_axis=1, concat_axis=0, tiled=True)
    frames = exchanged.shape[0]
    cycle_count = exchanged.shape[1]
    first_cycle = lax.axis_index("frame") * cycle_count
    own_member = lax.dynamic_slice_in_dim(member, first_cycle, cycle_count, 0)
    widened = exchanged.astype(jnp.float32)
    cycle_sums = jnp.transpose(jnp.sum(widened, axis=2), (1, 0))
    image = jnp.sum(widened, axis=0) / frames
    totals, pixel_sums = lax.psum((cycle_sums, jnp.sum(own_member, axis=1)), "tile")
    pixel_total = jnp.maximum(pixel_sums, 1.0)
    clamped = jnp.maximum(totals / pixel_total[:, None], 1.0)
    row_count = frames // lax.axis_size("tile")
    row_start = lax.axis_index("tile") * row_count
    gram_part = lax.psum_scatter(
        gram_block(exchanged, exchanged), "tile", scatter_dimension=0, tiled=True
    )
    row_clamped = lax.dynamic_slice_in_dim(clamped, row_start, row_count, 1)
    two_time = jnp.transpose(gram_part, (1, 0, 2)) / (
        pixel_total[:, None, None] * row_clamped[:, :, None] * clamped[:, None, :]
    )
    lag_total = jnp.maximum(lag_counts(age_bin, row_start, row_count), 1.0)
    whole_map = lax.all_gather(two_time, "tile", axis=1, tiled=True)
    band_sum = lax.dynamic_slice_in_dim(band_rows(whole_map, age_bin), row_start, row_count, 2)
    return (two_time, band_sum / lag_total[None], image[None])


def solution(mesh):
    in_specs = (
        P("frame", "tile"),
        P("tile"),
        P("tile"),
        P("tile"),
        P("tile"),
        P("tile", None, None),
        P(),
    )
    out_specs = (P("frame", "tile", None), P("frame", None, "tile"), P("tile", "frame", None))
    return jax.shard_map(local, mesh=mesh, in_specs=in_specs, out_specs=out_specs, check_vma=False)
```

profile of v0, /device:TPU:1, one launch (start us, length us, event | category | flops | bytes accessed | tf_op | source)
XLA Modules:
  0.0 456.4 jit_solution(15316091511293030886)
XLA Ops:
  7.2 0.0 copy-start
  7.2 0.0 reduce-scatter.2.cloned.1.call-start
  7.2 0.8 squeeze.8
  8.1 0.8 squeeze.9
  8.9 0.7 bitcast_compare_fusion
  9.6 11.8 %copy_bitcast_fusion = f32[32,1024,128]{2,0,1:T(8,128)} fusion(f32[32,131072]{1,0:T(8,128)} %param.11), kind=kLoop, calls=%fused_computation.7 | loop fusion | bytes 33554432 | tf_op jit(solution)/shard_map/reshape | solution.py:69
  21.4 18.1 %gather_fusion = f32[1024,32,128]{2,1,0:T(8,128)} fusion(f32[32,1024,128]{2,0,1:T(8,128)} %copy_bitcast_fusion, s32[1024]{0:T(1024)S(1)} %broadcast_clamp_fusion), kind=kCustom, calls=%fused_computation.4 | custom fusion | bytes 33558528 | tf_op jit(solution)/shard_map/jit(_take)/gather | solution.py:69
  39.6 14.1 %copy.25 = f32[32,1024,128]{2,1,0:T(8,128)} copy(f32[32,1024,128]{2,0,1:T(8,128)} %bitcast.63) | data formatting | bytes 33554432 | tf_op jit(solution)/shard_map/jit(_take)/gather | solution.py:69
  53.7 18.3 %gather.13 = f32[32,32,4096]{2,1,0:T(8,128)} reshape(f32[32,1024,128]{2,1,0:T(8,128)} %copy.25) | data formatting | bytes 33554432 | tf_op jit(solution)/shard_map/jit(_take)/gather | solution.py:69
  72.0 2.8 gather_fusion.1
  74.8 2.8 gather_fusion.4
  77.6 0.1 eq.39
  77.7 2.8 gather_fusion.3
  80.5 2.8 gather_fusion.2
  83.3 0.9 broadcast_select_fusion.1
  84.3 0.1 mul.65
  84.4 0.1 sub.11
  84.5 0.2 broadcast_in_dim.79
  84.7 0.1 copy.41
  84.8 9.5 %multiply_convert_fusion = bf16[32,32,4096]{2,1,0:T(8,128)(2,1)} fusion(f32[32,32,4096]{2,1,0:T(8,128)} %gather.13, f32[32,4096]{1,0:T(8,128)S(1)} %mul.65, f32[32,4096]{1,0:T(8,128)S(1)} %sub.11, pred[32,4096]{1,0:T(8,128)(4,1)S(1)} %bitcast.69), kind=kLoop, calls=%fused_computation.8 | loop fusion | flops 16777216 | bytes 26345472 | tf_op jit(solution)/shard_map/convert_element_type | solution.py:72
  94.2 11.2 %copy.26 = bf16[32,32,4096]{2,0,1:T(8,128)(2,1)} copy(bf16[32,32,4096]{2,1,0:T(8,128)(2,1)} %multiply_convert_fusion) | data formatting | bytes 16777216 | tf_op jit(solution)/shard_map/convert_element_type | solution.py:72
  105.4 104.3 %all_to_all.15 = bf16[32,32,4096]{2,0,1:T(8,128)(2,1)S(1)} all-to-all(bf16[32,32,4096]{2,0,1:T(8,128)(2,1)} %copy.26), channel_id=1, replica_groups=mesh['frame'=32,'tile'=4] {'frame'}, dimensions={1} | all-to-all | bytes 16777216 | tf_op jit(solution)/shard_map/all_to_all | solution.py:75
  209.7 3.2 copy-done.2
  212.9 10.4 %convolution_bitcast_fusion = f32[1024,1,1024]{0,2,1:T(8,128)} fusion(bf16[1024,4096]{1,0:T(8,128)(2,1)S(1)} %bitcast.65), kind=kOutput, calls=%fused_computation.13 | convolution fusion | flops 8589934592 | bytes 12582912 | tf_op jit(solution)/shard_map/irp,jrp->irj/dot_general | solution.py:37
  223.3 0.0 reduce-scatter.2.cloned.1.call-update
  223.3 0.0 all-gather.2.cloned.1.call-start
  223.4 0.2 broadcast_select_fusion
  223.6 0.1 convert_element_type.25
  223.7 0.1 reshape.229
  223.8 0.2 broadcast_in_dim.87
  224.0 0.1 copy.40
  224.1 0.7 fusion.7
  224.8 7.8 %convert_reduce_fusion = (f32[4096]{0:T(1024)S(1)}, f32[32,32]{1,0:T(8,128)S(1)}) fusion(bf16[32,32,4096]{2,0,1:T(8,128)(2,1)} %copy-done.2), kind=kLoop, calls=%fused_computation.5 | loop fusion | flops 12577792 | bytes 8409088 | tf_op jit(solution)/shard_map/reduce_sum | solution.py:82
  232.6 0.1 transpose.25
  232.7 12.1 %all-reduce.2 = (f32[1,1024]{1,0:T(1,128)S(1)}, f32[1]{0:T(128)}) all-reduce(f32[1,1024]{1,0:T(1,128)S(1)} %transpose.25, f32[1]{0:T(128)} %bitcast.13), channel_id=1, replica_groups=mesh['frame'=32,'tile'=4] {'tile'}, use_global_device_ids=true, to_apply=%region_4.7 | all-reduce | flops 1025 | bytes 8200 | tf_op jit(solution)/shard_map/psum | solution.py:83
  245.5 23.8 %reduce-scatter.2.cloned.1.call-done = f32[256,1,1024]{0,2,1:T(8,128)} async-done(((f32[1024,1,1024]{0,2,1:T(8,128)}), f32[256,1,1024]{0,2,1:T(8,128)}) %reduce-scatter.2.cloned.1.call-update) | async-done | bytes 1048592 | tf_op jit(solution)/shard_map/reduce_scatter | solution.py:88
  269.3 2.4 bitcast_divide_fusion
  271.7 0.0 all-gather.2.cloned.1.call-update
  271.7 0.6 broadcast_multiply_fusion
  272.3 2.5 copy.30
  274.9 44.7 %all-gather.2.cloned.1.call-done = f32[1,1024,1024]{1,2,0:T(8,128)} async-done(((f32[1,256,1024]{1,2,0:T(8,128)}), f32[1,1024,1024]{1,2,0:T(8,128)}) %all-gather.2.cloned.1.call-update) | async-done | bytes 4194320 | tf_op jit(solution)/shard_map/all_gather | solution.py:96
  319.6 5.4 %copy.32 = f32[1,1024,1024]{2,1,0:T(8,128)} copy(f32[1,1024,1024]{1,2,0:T(8,128)} %all-gather.2.cloned.1.call-done) | data formatting | bytes 8388608
  325.0 3.3 pad_bitcast_fusion
  328.2 12.5 %copy.36 = f32[1,1,1024,2048]{3,1,2,0:T(1,128)} copy(f32[1,1,1024,2048]{3,2,1,0:T(8,128)S(1)} %pad_bitcast_fusion) | data formatting | bytes 16777216
  340.8 91.3 %pad_reduce_fusion = f32[2098176]{0:T(1024)} fusion(f32[1,2097152]{1,0:T(1,128)} %bitcast.64), kind=kLoop, calls=%fused_computation.9 | loop fusion | bytes 16781312 | tf_op jit(solution)/shard_map/concatenate | solution.py:14
  432.1 12.9 %reshape.231 = f32[1,1024,2049]{2,1,0:T(8,128)} reshape(f32[2098176]{0:T(1024)} %pad_reduce_fusion) | data formatting | bytes 16785408 | tf_op jit(solution)/shard_map/reshape | solution.py:21
  445.0 3.6 fusion
  448.6 0.9 fusion.2
  (20 shorter events, 0.1 us)
Async XLA Ops:
  7.2 64.8 %copy-start = (f32[131072]{0:T(1024)S(1)}, f32[131072]{0:T(1024)}, u32[]{:S(2)}) copy-start(f32[131072]{0:T(1024)} %param.12) | copy-start | bytes 1572868
  7.2 262.1 %reduce-scatter.2.cloned.1.call-start = ((), (), s32[]{:S(2)}) async-start(), calls=%async_computation.2 | async-start | bytes 5242880 | tf_op jit(solution)/shard_map/reduce_scatter | solution.py:88
  53.7 21.1 %copy-start.3 = (s32[131072]{0:T(1024)S(1)}, s32[131072]{0:T(1024)}, u32[]{:S(2)}) copy-start(s32[131072]{0:T(1024)} %param.14) | copy-start | bytes 1572868
  72.0 5.7 %copy-start.4 = (s32[131072]{0:T(1024)S(1)}, s32[131072]{0:T(1024)}, u32[]{:S(2)}) copy-start(s32[131072]{0:T(1024)} %param.15) | copy-start | bytes 1572868
  72.0 8.6 %copy-start.5 = (f32[131072]{0:T(1024)S(1)}, f32[131072]{0:T(1024)}, u32[]{:S(2)}) copy-start(f32[131072]{0:T(1024)} %param.13) | copy-start | bytes 1572868
  209.7 3.2 copy-start.2
  223.3 96.3 %all-gather.2.cloned.1.call-start = ((), (), s32[]{:S(2)}) async-start(), calls=%async_computation.3 | async-start | bytes 5242880 | tf_op jit(solution)/shard_map/all_gather | solution.py:96
  340.8 108.8 %copy-start.1 = (f32[131072]{0:T(1024)S(1)}, f32[131072]{0:T(1024)}, u32[]{:S(2)}) copy-start(f32[131072]{0:T(1024)} %param.12) | copy-start | bytes 1572868
  432.1 12.9 %copy-start.6 = (s32[1024]{0:T(1024)S(1)}, s32[1024]{0:T(1024)}, u32[]{:S(2)}) copy-start(s32[1024]{0:T(1024)} %param.17) | copy-start | bytes 12292
Sparse Core Ops, SparseCore 0:
  223.4 45.8 reduce-scatter.1
  271.9 47.7 all-gather.1
where the time goes:
time: 458 us; the launch traced here: 456 us
  local copies, waits for them, and re-layouts  219 us (48%)
  blocking collectives  116 us (25%)
  waiting for transfers between devices  68.6 us (15%)
  other arithmetic  22.9 us (5%)
  matrix products  15 us (3%)
  between operations  14.9 us (3%)
    all_to_all x1, blocking collectives, local(): lax.all_to_all(sorted_frames, 'frame', split_axis=1, concat_axis=0, tiled...  104 us
    concatenate x1, local copies, waits for them, and re-layouts, band_rows(): jnp.concatenate([padded_map.reshape(cycle_count, row_count * span), jnp.z...  91.3 us
    gather x3, local copies, waits for them, and re-layouts, local(): jnp.take(counts.reshape(frame_part, block_total, BLK), block_ids, axis=1)  50.5 us
    all_gather x1, waiting for transfers between devices, local(): whole_map = lax.all_gather(two_time, 'tile', axis=1, tiled=True)  44.7 us
    unnamed x20, local copies, waits for them, and re-layouts  27.1 us
    reduce_scatter x1, waiting for transfers between devices, local(): lax.psum_scatter(gram_block(exchanged, exchanged), 'tile', scatter_dimens...  23.8 us
    reshape x1, local copies, waits for them, and re-layouts, band_rows(): flattened.reshape(cycle_count, row_count, span + 1)[:, :, :col_width]  12.9 us
    psum x1, blocking collectives, local(): lax.psum((cycle_sums, jnp.sum(own_member, axis=1)), 'tile')  12.1 us
  transfers between devices with their start and end apart: 2, of which 2 were waited for; matrix products, arithmetic and copies ran while one was open for 3% of the time, Pallas kernels for 0%

commit v1 on v0

--- a/solution.py
+++ b/solution.py
@@ -93,7 +93,9 @@
         pixel_total[:, None, None] * row_clamped[:, :, None] * clamped[:, None, :]
     )
     lag_total = jnp.maximum(lag_counts(age_bin, row_start, row_count), 1.0)
-    whole_map = lax.all_gather(two_time, "tile", axis=1, tiled=True)
+    whole_map = jnp.concatenate(
+        lax.all_to_all(jnp.stack([two_time] * lax.axis_size("tile")), "tile", 0, 0), axis=1
+    )
     band_sum = lax.dynamic_slice_in_dim(band_rows(whole_map, age_bin), row_start, row_count, 2)
     return (two_time, band_sum / lag_total[None], image[None])
 

time: 458 us -> 460 us (level)
  starting transfers between devices: 0.08 us -> 5.1 us
    all_to_all x0 -> x1, waiting for transfers between devices: none -> 45.9 us  [local(): lax.all_to_all(jnp.stack([two_time] * lax.axis_size('tile')), 'tile', 0, 0)]
    all_gather x1 -> x0, waiting for transfers between devices: 44.7 us -> none  [local(): whole_map = lax.all_gather(two_time, 'tile', axis=1, tiled=True)]
    unnamed x20 -> x21, local copies, waits for them, and re-layouts: 27.1 us -> 20.5 us
    all_to_all x0 -> x1, starting transfers between devices: none -> 5.06 us  [local(): lax.all_to_all(jnp.stack([two_time] * lax.axis_size('tile')), 'tile', 0, 0)]
  transfers between devices with their start and end apart: 2 -> 2, of which waited for: 2 -> 2; matrix products, arithmetic and copies ran while one was open for 3% -> 2% of each run, Pallas kernels for 0% -> 0%
where the time goes in v1:
time: 460 us; the launch traced here: 458 us
  local copies, waits for them, and re-layouts  215 us (47%)
  blocking collectives  116 us (25%)
  waiting for transfers between devices  70 us (15%)
  other arithmetic  22.1 us (5%)
  matrix products  15 us (3%)
  between operations  14.9 us (3%)
  starting transfers between devices  5.1 us (1%)
    all_to_all x1, blocking collectives, local(): lax.all_to_all(sorted_frames, 'frame', split_axis=1, concat_axis=0, tiled...  104 us
    concatenate x1, local copies, waits for them, and re-layouts, band_rows(): jnp.concatenate([padded_map.reshape(cycle_count, row_count * span), jnp.z...  91.3 us
    gather x3, local copies, waits for them, and re-layouts, local(): jnp.take(counts.reshape(frame_part, block_total, BLK), block_ids, axis=1)  50.5 us
    all_to_all x1, waiting for transfers between devices, local(): lax.all_to_all(jnp.stack([two_time] * lax.axis_size('tile')), 'tile', 0, 0)  45.9 us
    reduce_scatter x1, waiting for transfers between devices, local(): lax.psum_scatter(gram_block(exchanged, exchanged), 'tile', scatter_dimens...  24.1 us
    unnamed x21, local copies, waits for them, and re-layouts  20.5 us
    reshape x1, local copies, waits for them, and re-layouts, band_rows(): flattened.reshape(cycle_count, row_count, span + 1)[:, :, :col_width]  12.9 us
    psum x1, blocking collectives, local(): lax.psum((cycle_sums, jnp.sum(own_member, axis=1)), 'tile')  11.9 us
  transfers between devices with their start and end apart: 2, of which 2 were waited for; matrix products, arithmetic and copies ran while one was open for 2% of the time, Pallas kernels for 0%

profile of v1, /device:TPU:1, one launch (start us, length us, event | category | flops | bytes accessed | tf_op | source)
XLA Modules:
  0.0 458.1 jit_solution(3572855804712538275)
XLA Ops:
  7.2 0.0 reduce-scatter.2.cloned.1.call-start
  7.2 0.8 squeeze.8
  8.1 0.8 squeeze.9
  8.9 0.7 bitcast_compare_fusion
  9.6 11.8 %copy_bitcast_fusion = f32[32,1024,128]{2,0,1:T(8,128)} fusion(f32[32,131072]{1,0:T(8,128)} %param.11), kind=kLoop, calls=%fused_computation.7 | loop fusion | bytes 33554432 | tf_op jit(solution)/shard_map/reshape | solution.py:69
  21.4 18.1 %gather_fusion = f32[1024,32,128]{2,1,0:T(8,128)} fusion(f32[32,1024,128]{2,0,1:T(8,128)} %copy_bitcast_fusion, s32[1024]{0:T(1024)S(1)} %broadcast_clamp_fusion), kind=kCustom, calls=%fused_computation.4 | custom fusion | bytes 33558528 | tf_op jit(solution)/shard_map/jit(_take)/gather | solution.py:69
  39.6 14.1 %copy.26 = f32[32,1024,128]{2,1,0:T(8,128)} copy(f32[32,1024,128]{2,0,1:T(8,128)} %bitcast.66) | data formatting | bytes 33554432 | tf_op jit(solution)/shard_map/jit(_take)/gather | solution.py:69
  53.7 18.3 %gather.13 = f32[32,32,4096]{2,1,0:T(8,128)} reshape(f32[32,1024,128]{2,1,0:T(8,128)} %copy.26) | data formatting | bytes 33554432 | tf_op jit(solution)/shard_map/jit(_take)/gather | solution.py:69
  72.0 2.8 gather_fusion.1
  74.8 2.8 gather_fusion.4
  77.6 0.1 eq.39
  77.7 2.8 gather_fusion.3
  80.5 2.8 gather_fusion.2
  83.3 0.9 broadcast_select_fusion.1
  84.3 0.1 mul.74
  84.4 0.1 sub.11
  84.5 0.2 broadcast_in_dim.79
  84.7 0.1 copy.41
  84.8 9.5 %multiply_convert_fusion = bf16[32,32,4096]{2,1,0:T(8,128)(2,1)} fusion(f32[32,32,4096]{2,1,0:T(8,128)} %gather.13, f32[32,4096]{1,0:T(8,128)S(1)} %mul.74, f32[32,4096]{1,0:T(8,128)S(1)} %sub.11, pred[32,4096]{1,0:T(8,128)(4,1)S(1)} %bitcast.72), kind=kLoop, calls=%fused_computation.8 | loop fusion | flops 16777216 | bytes 26345472 | tf_op jit(solution)/shard_map/convert_element_type | solution.py:72
  94.2 11.2 %copy.27 = bf16[32,32,4096]{2,0,1:T(8,128)(2,1)} copy(bf16[32,32,4096]{2,1,0:T(8,128)(2,1)} %multiply_convert_fusion) | data formatting | bytes 16777216 | tf_op jit(solution)/shard_map/convert_element_type | solution.py:72
  105.4 104.3 %all_to_all.20 = bf16[32,32,4096]{2,0,1:T(8,128)(2,1)S(1)} all-to-all(bf16[32,32,4096]{2,0,1:T(8,128)(2,1)} %copy.27), channel_id=1, replica_groups=mesh['frame'=32,'tile'=4] {'frame'}, dimensions={1} | all-to-all | bytes 16777216 | tf_op jit(solution)/shard_map/all_to_all | solution.py:75
  209.7 3.2 copy-done.2
  212.9 10.4 %convolution_bitcast_fusion = f32[1024,1,1024]{0,2,1:T(8,128)} fusion(bf16[1024,4096]{1,0:T(8,128)(2,1)S(1)} %bitcast.68), kind=kOutput, calls=%fused_computation.13 | convolution fusion | flops 8589934592 | bytes 12582912 | tf_op jit(solution)/shard_map/irp,jrp->irj/dot_general | solution.py:37
  223.3 0.0 reduce-scatter.2.cloned.1.call-update
  223.3 0.2 broadcast_select_fusion
  223.5 0.1 convert_element_type.25
  223.6 0.1 reshape.257
  223.8 0.2 broadcast_in_dim.87
  224.0 0.1 copy.40
  224.0 0.7 fusion.7
  224.7 7.8 %convert_reduce_fusion = (f32[4096]{0:T(1024)S(1)}, f32[32,32]{1,0:T(8,128)S(1)}) fusion(bf16[32,32,4096]{2,0,1:T(8,128)(2,1)} %copy-done.2), kind=kLoop, calls=%fused_computation.5 | loop fusion | flops 12577792 | bytes 8409088 | tf_op jit(solution)/shard_map/reduce_sum | solution.py:82
  232.6 0.1 transpose.27
  232.6 11.9 %all-reduce.2 = (f32[1,1024]{1,0:T(1,128)S(1)}, f32[1]{0:T(128)}) all-reduce(f32[1,1024]{1,0:T(1,128)S(1)} %transpose.27, f32[1]{0:T(128)} %bitcast.13), channel_id=1, replica_groups=mesh['frame'=32,'tile'=4] {'tile'}, use_global_device_ids=true, to_apply=%region_4.7 | all-reduce | flops 1025 | bytes 8200 | tf_op jit(solution)/shard_map/psum | solution.py:83
  245.2 24.1 %reduce-scatter.2.cloned.1.call-done = f32[256,1,1024]{0,2,1:T(8,128)} async-done(((f32[1024,1,1024]{0,2,1:T(8,128)}), f32[256,1,1024]{0,2,1:T(8,128)}) %reduce-scatter.2.cloned.1.call-update) | async-done | bytes 1048592 | tf_op jit(solution)/shard_map/reduce_scatter | solution.py:88
  269.3 1.4 bitcast_divide_fusion
  270.7 0.3 copy.30
  271.1 2.5 stack.2
  273.6 5.1 %all-to-all-start.1 = ((f32[4,1,256,1024]{3,2,1,0:T(8,128)}), f32[4,1,256,1024]{3,2,1,0:T(8,128)}, u32[]{:S(2)}, u32[]{:S(2)}) async-start(f32[4,1,256,1024]{3,2,1,0:T(8,128)} %stack.2), calls=%async_computation.2 | async-start | bytes 8388608 | tf_op jit(solution)/shard_map/all_to_all | solution.py:97
  278.7 0.6 broadcast_multiply_fusion
  279.3 0.2 bitcast_divide_fusion.1
  279.5 1.3 copy.31
  280.8 45.9 %all-to-all-done.1 = f32[4,1,256,1024]{3,2,1,0:T(8,128)} async-done(((f32[4,1,256,1024]{3,2,1,0:T(8,128)}), f32[4,1,256,1024]{3,2,1,0:T(8,128)}, u32[]{:S(2)}, u32[]{:S(2)}) %all-to-all-start.1) | async-done | bytes 4194336 | tf_op jit(solution)/shard_map/all_to_all | solution.py:97
  326.7 3.3 pad_bitcast_fusion
  329.9 12.5 %copy.36 = f32[1,1,1024,2048]{3,1,2,0:T(1,128)} copy(f32[1,1,1024,2048]{3,2,1,0:T(8,128)S(1)} %pad_bitcast_fusion) | data formatting | bytes 16777216
  342.5 91.3 %pad_reduce_fusion = f32[2098176]{0:T(1024)} fusion(f32[1,2097152]{1,0:T(1,128)} %bitcast.67), kind=kLoop, calls=%fused_computation.9 | loop fusion | bytes 16781312 | tf_op jit(solution)/shard_map/concatenate | solution.py:14
  433.8 12.9 %reshape.260 = f32[1,1024,2049]{2,1,0:T(8,128)} reshape(f32[2098176]{0:T(1024)} %pad_reduce_fusion) | data formatting | bytes 16785408 | tf_op jit(solution)/shard_map/reshape | solution.py:21
  446.7 3.6 fusion
  450.3 0.9 fusion.2
  (23 shorter events, 0.1 us)
Async XLA Ops:
  7.2 64.8 %copy-start = (f32[131072]{0:T(1024)S(1)}, f32[131072]{0:T(1024)}, u32[]{:S(2)}) copy-start(f32[131072]{0:T(1024)} %param.12) | copy-start | bytes 1572868
  7.2 262.1 %reduce-scatter.2.cloned.1.call-start = ((), (), s32[]{:S(2)}) async-start(), calls=%async_computation.3 | async-start | bytes 5242880 | tf_op jit(solution)/shard_map/reduce_scatter | solution.py:88
  53.7 21.1 %copy-start.3 = (s32[131072]{0:T(1024)S(1)}, s32[131072]{0:T(1024)}, u32[]{:S(2)}) copy-start(s32[131072]{0:T(1024)} %param.14) | copy-start | bytes 1572868
  72.0 5.7 %copy-start.4 = (s32[131072]{0:T(1024)S(1)}, s32[131072]{0:T(1024)}, u32[]{:S(2)}) copy-start(s32[131072]{0:T(1024)} %param.15) | copy-start | bytes 1572868
  72.0 8.6 %copy-start.5 = (f32[131072]{0:T(1024)S(1)}, f32[131072]{0:T(1024)}, u32[]{:S(2)}) copy-start(f32[131072]{0:T(1024)} %param.13) | copy-start | bytes 1572868
  209.7 3.2 copy-start.2
  271.1 8.2 %copy-start.6 = (f32[256,1,1024]{0,2,1:T(8,128)S(1)}, f32[256,1,1024]{0,2,1:T(8,128)}, u32[]{:S(2)}) copy-start(f32[256,1,1024]{0,2,1:T(8,128)} %reduce-scatter.2.cloned.1.call-done) | copy-start | bytes 3145732
  273.6 53.1 %all-to-all-start.1 = ((f32[4,1,256,1024]{3,2,1,0:T(8,128)}), f32[4,1,256,1024]{3,2,1,0:T(8,128)}, u32[]{:S(2)}, u32[]{:S(2)}) async-start(f32[4,1,256,1024]{3,2,1,0:T(8,128)} %stack.2), calls=%async_computation.2 | async-start | bytes 8388608 | tf_op jit(solution)/shard_map/all_to_all | solution.py:97
  342.5 108.8 %copy-start.1 = (f32[131072]{0:T(1024)S(1)}, f32[131072]{0:T(1024)}, u32[]{:S(2)}) copy-start(f32[131072]{0:T(1024)} %param.12) | copy-start | bytes 1572868
  433.8 12.9 %copy-start.7 = (s32[1024]{0:T(1024)S(1)}, s32[1024]{0:T(1024)}, u32[]{:S(2)}) copy-start(s32[1024]{0:T(1024)} %param.17) | copy-start | bytes 12292
Sparse Core Ops, SparseCore 0:
  223.4 45.8 reduce-scatter.1
